TPU v7x, 512 devices: a whole 4x4x16 slice. The times are simulated.
512 devices in a mesh: band: 64 (over x_lo, z, core), tile: 8 (over y, x_hi).
Axes of the slice: x: 4 (x_hi: 2, x_lo: 2; x = x_hi * 2 + x_lo), y: 4, z: 16, core: 2. Of those that a mesh axis runs over, the one named last changes fastest.
Arguments:
- alm: bfloat16 [1024, 9, 2, 1024], P('band', None, None, 'tile'), may hold values from -22 to 22
- legendre: bfloat16 [1024, 1024, 1024], P('band', 'tile'), may hold values from -0.1875 to 0.1875
- order_of_slot: int32 [1024], replicated, may hold values from 0 to 1023, each once
Outputs:
- ilc_map: float32 [1024, 4096], P('band', 'tile')
- ilc_alm: float32 [1024, 2, 1024], P('band', None, 'tile')
Inputs may be any that keep to these rules, and one draw needn't show every extreme that they name: `order_of_slot`: every order 0 to 1023 stands in exactly one slot.
All inputs are finite; a program needn't handle non-finite values.
Results may differ from a plain program's by a relative error of at most 0.02.
Values may be sent and summed in bfloat16 or wider, within the bound.
A program may use at most 64 MiB of HBM per device.

v0:
```python
import math
import jax
import jax.numpy as jnp
from jax import lax
from jax.sharding import PartitionSpec as P

C = 9
L = 1024
NLON = 4096
RB = 16
HALO = 32
RIDGE = 0.1
EPSILON = 1e-06


def sent_to_all(value, axis):
    copies = jnp.broadcast_to(value, (lax.axis_size(axis), *value.shape))
    return lax.all_to_all(copies, axis, split_axis=0, concat_axis=0, tiled=True)


def taken_together(value, axis):
    return sent_to_all(value, axis).astype(jnp.float32).sum(axis=0)


def with_halo(block, sides, width):
    for axis, dim in sides:
        count = lax.axis_size(axis)
        forward = [(i, i + 1) for i in range(count - 1)]
        forward.append((count - 1, 0))
        backward = [(target, source) for source, target in forward]
        low = lax.ppermute(
            lax.slice_in_dim(block, block.shape[dim] - width, None, axis=dim), axis, forward
        )
        high = lax.ppermute(lax.slice_in_dim(block, 0, width, axis=dim), axis, backward)
        block = jnp.concatenate([low, block, high], axis=dim)
    return block


def taken_together_2(value, axis):
    everything = sent_to_all(value, axis)
    return jnp.sum(everything, axis=0)


def make_basis(order_of_slot, begin_at, cell_count):
    columns = begin_at + jnp.arange(cell_count, dtype=jnp.int32)
    phases = order_of_slot[:, None] * columns[None, :] % NLON
    angles = phases.astype(jnp.float32) * (2.0 * math.pi / NLON)
    scaling = 1.0 / math.sqrt(L)
    return jnp.stack([jnp.cos(angles) * scaling, -jnp.sin(angles) * scaling]).astype(jnp.bfloat16)


def pair_table():
    return [(a_at, b_at) for a_at in range(C) for b_at in range(a_at, C)]


def window_sum(products):
    span_cells = products.shape[2]
    width_cells = span_cells - 2 * HALO
    total = products
    span = 1
    while span < 2 * HALO:
        total = total[:, :, :-span] + total[:, :, span:]
        span = span * 2
    return total[:, :, :width_cells] + products[:, :, 2 * HALO : 2 * HALO + width_cells]


def smooth_pairs(padded):
    widened = padded.astype(jnp.float32)
    products = jnp.stack([widened[a_at] * widened[b_at] for a_at, b_at in pair_table()])
    return window_sum(products) / (2 * HALO + 1)


def solve_weights(smoothed):
    entries = {}
    for pair_at, (a_at, b_at) in enumerate(pair_table()):
        entries[a_at, b_at] = smoothed[pair_at]
    trace_mean = entries[0, 0]
    for chan_at in range(1, C):
        trace_mean = trace_mean + entries[chan_at, chan_at]
    ridge_term = RIDGE * (trace_mean / C + EPSILON)
    factor = {}
    for row_at in range(C):
        for col_at in range(row_at + 1):
            running = entries[col_at, row_at]
            if row_at == col_at:
                running = running + ridge_term
            for inner_at in range(col_at):
                running = running - factor[row_at, inner_at] * factor[col_at, inner_at]
            if row_at == col_at:
                factor[row_at, row_at] = jnp.sqrt(running)
            else:
                factor[row_at, col_at] = running / factor[col_at, col_at]
    forward = []
    for row_at in range(C):
        running = jnp.ones_like(ridge_term)
        for inner_at in range(row_at):
            running = running - factor[row_at, inner_at] * forward[inner_at]
        forward.append(running / factor[row_at, row_at])
    backward = [forward[0]] * C
    for row_at in reversed(range(C)):
        running = forward[row_at]
        for inner_at in range(row_at + 1, C):
            running = running - factor[inner_at, row_at] * backward[inner_at]
        backward[row_at] = running / factor[row_at, row_at]
    normal = backward[0]
    for chan_at in range(1, C):
        normal = normal + backward[chan_at]
    return jnp.stack([solved / normal for solved in backward])


def to_band_layout(parts):
    return lax.all_to_all(parts, "band", split_axis=3, concat_axis=0, tiled=True)


def body(alm, legendre, order_of_slot):
    tile_count = lax.axis_size("tile")
    band_count = lax.axis_size("band")
    tile_at = lax.axis_index("tile")
    slot_count = alm.shape[0]
    lon_cells = NLON // tile_count
    partial_value = jnp.einsum("scel,slr->scer", alm, legendre, preferred_element_type=jnp.float32)
    own_basis = make_basis(order_of_slot, tile_at * lon_cells, lon_cells)
    shaped = partial_value.astype(jnp.bfloat16).reshape(slot_count, C, 2, band_count, RB)
    gathered = to_band_layout(shaped)
    summed = taken_together(gathered.astype(jnp.float32).astype(jnp.bfloat16), "tile").astype(
        jnp.float32
    )
    cycle_modes = summed.astype(jnp.bfloat16).reshape(L, C, 2, RB)
    channel_maps = jnp.einsum(
        "scer,esx->crx", cycle_modes, own_basis, preferred_element_type=jnp.float32
    ).astype(jnp.bfloat16)
    padded = with_halo(channel_maps, (("tile", 2),), HALO)
    weights = solve_weights(smooth_pairs(padded))
    ilc_map = jnp.sum(weights * channel_maps.astype(jnp.float32), axis=0)
    map_low = ilc_map.astype(jnp.bfloat16)
    cycle_partial = jnp.einsum(
        "rx,esx->res", map_low, own_basis, preferred_element_type=jnp.float32
    )
    routed = lax.all_to_all(cycle_partial, "band", split_axis=2, concat_axis=0, tiled=True)
    cycle_spectra = taken_together_2(routed, "tile").astype(jnp.bfloat16)
    ilc_alm = jnp.einsum(
        "slr,res->sel", legendre, cycle_spectra, preferred_element_type=jnp.float32
    )
    return (ilc_map, ilc_alm)


def solution(mesh):
    placed = (P("band", None, None, "tile"), P("band", "tile", None), P())
    return jax.shard_map(
        body,
        mesh=mesh,
        in_specs=placed,
        out_specs=(P("band", "tile"), P("band", None, "tile")),
        check_vma=False,
    )
```

profile of v0, /device:TPU:1, one launch (start us, length us, event | category | flops | bytes accessed | tf_op | source)
XLA Modules:
  0.0 249.8 jit_solution(7399007213763697263)
XLA Ops:
  0.6 2.9 %fusion.7 = bf16[16,9,2,1024]{3,1,2,0:T(8,128)(2,1)S(1)} fusion(bf16[16,128,1024]{2,1,0:T(8,128)(2,1)} %param.4, bf16[16,9,2,128]{3,2,1,0:T(2,128)(2,1)} %param.3), kind=kOutput, calls=%fused_computation.20 | convolution fusion | flops 75792384 | bytes 4857856 | tf_op jit(solution)/shard_map/scel,slr->scer/dot_general | solution.py:121
  3.5 4.9 %reshape.154 = bf16[16,9,2,64,16]{4,3,1,2,0:T(8,128)(2,1)} reshape(bf16[16,9,2,1024]{3,1,2,0:T(8,128)(2,1)S(1)} %fusion.7) | data formatting | bytes 1179648 | tf_op jit(solution)/shard_map/reshape | solution.py:123
  8.5 7.5 %copy.40 = bf16[16,9,2,64,16]{4,0,2,1,3:T(8,128)(2,1)} copy(bf16[16,9,2,64,16]{4,3,1,2,0:T(8,128)(2,1)} %reshape.154) | data formatting | bytes 1179648 | tf_op jit(solution)/shard_map/reshape | solution.py:123
  16.0 6.6 %reshape.155 = bf16[64,2,2304]{2,1,0:T(2,128)(2,1)S(1)} reshape(bf16[64,9,2,16,16]{4,3,2,1,0:T(8,128)(2,1)} %bitcast.50) | data formatting | bytes 1179648
  22.6 52.0 %all_to_all.46 = bf16[64,2,2304]{2,1,0:T(2,128)(2,1)S(1)} all-to-all(bf16[64,2,2304]{2,1,0:T(2,128)(2,1)S(1)} %reshape.155), channel_id=1, replica_groups=mesh['band'=64,'tile'=8] {'band'}, dimensions={0} | all-to-all | bytes 1179648 | tf_op jit(solution)/shard_map/all_to_all | solution.py:112
  74.7 4.7 %reshape.156 = bf16[64,9,2,16,16]{4,3,2,1,0:T(8,128)(2,1)} reshape(bf16[64,2,2304]{2,1,0:T(2,128)(2,1)S(1)} %all_to_all.46) | data formatting | bytes 1179648
  79.4 5.3 %bitcast_bitcast_fusion = bf16[64,16,9,2,1,16]{5,1,3,2,0,4:T(8,128)(2,1)} fusion(bf16[64,9,2,16,16]{4,3,2,1,0:T(8,128)(2,1)} %reshape.156), kind=kLoop, calls=%fused_computation.250 | loop fusion | bytes 1179648 | tf_op jit(solution)/shard_map/all_to_all | solution.py:112
  84.7 9.8 %copy.22 = bf16[64,16,9,2,1,16]{1,0,5,3,2,4:T(8,128)(2,1)} copy(bf16[64,16,9,2,1,16]{5,1,3,2,0,4:T(8,128)(2,1)} %bitcast_bitcast_fusion) | data formatting | bytes 1179648 | tf_op jit(solution)/shard_map/all_to_all | solution.py:112
  94.5 8.9 %all_to_all.35 = bf16[1024,9,2,16]{0,3,2,1:T(8,128)(2,1)S(1)} reshape(bf16[64,16,9,2,1,16]{1,0,5,3,2,4:T(8,128)(2,1)} %copy.22) | data formatting | bytes 1179648 | tf_op jit(solution)/shard_map/all_to_all | solution.py:112
  103.3 2.8 %broadcast_in_dim.8 = bf16[8,1024,9,2,1,16]{1,5,4,3,2,0:T(8,128)(2,1)} broadcast(bf16[1024,9,2,16]{0,3,2,1:T(8,128)(2,1)S(1)} %all_to_all.35), dimensions={1,2,3,5} | broadcast | bytes 5308416 | tf_op jit(solution)/shard_map/broadcast_in_dim | solution.py:17
  106.1 6.5 %all-to-all-start.1 = ((bf16[8,1024,9,2,1,16]{1,5,4,3,2,0:T(8,128)(2,1)}), bf16[8,1024,9,2,1,16]{1,5,4,3,2,0:T(8,128)(2,1)}, u32[]{:S(2)}, u32[]{:S(2)}) async-start(bf16[8,1024,9,2,1,16]{1,5,4,3,2,0:T(8,128)(2,1)} %broadcast_in_dim.8), calls=%async_computation.1 | async-start | bytes 9437184 | tf_op jit(solution)/shard_map/all_to_all | solution.py:18
  112.6 9.2 %multiply_convert_fusion.1 = (bf16[1,1024,512]{2,1,0:T(8,128)(2,1)S(1)}, bf16[1,1024,512]{2,1,0:T(8,128)(2,1)S(1)}) fusion(s32[512]{0:T(512)S(1)} %iota_add_fusion, s32[1024]{0:T(1024)S(1)} %copy-done.1), kind=kLoop, calls=%fused_computation.14 | loop fusion | flops 9961472 | bytes 2103296 | tf_op jit(solution)/shard_map/convert.1
  121.8 47.6 %all-to-all-done.1 = bf16[8,1024,9,2,1,16]{1,5,4,3,2,0:T(8,128)(2,1)} async-done(((bf16[8,1024,9,2,1,16]{1,5,4,3,2,0:T(8,128)(2,1)}), bf16[8,1024,9,2,1,16]{1,5,4,3,2,0:T(8,128)(2,1)}, u32[]{:S(2)}, u32[]{:S(2)}) %all-to-all-start.1) | async-done | bytes 4718624 | tf_op jit(solution)/shard_map/all_to_all | solution.py:18
  169.4 3.4 %reduce_sum.30 = bf16[1024,9,2,16]{0,3,2,1:T(8,128)(2,1)S(1)} reduce(bf16[8,1024,9,2,1,16]{1,5,4,3,2,0:T(8,128)(2,1)} %all-to-all-done.1, bf16[]{:T(256)} %constant.12.clone.1), dimensions={0,4}, to_apply=%region_0.1 | reduce | flops 2064384 | bytes 5308418 | tf_op jit(solution)/shard_map/reduce_sum | solution.py:22
  172.8 0.5 fusion.15
  173.3 0.1 fusion.121
  173.4 3.3 %collective-permute-start.1 = (bf16[9,16,32]{2,1,0:T(8,128)(2,1)S(1)}, bf16[9,16,32]{2,1,0:T(8,128)(2,1)S(1)}, u32[]{:S(2)}, u32[]{:S(2)}) collective-permute-start(bf16[9,16,32]{2,1,0:T(8,128)(2,1)S(1)} %get-tuple-element.14), channel_id=1, source_target_pairs={{1,0},{2,1},{3,2},{4,3},{5,4},{6,5},{7,6},{0,7},{9,8},{10,9},{11,1... | collective-permute-start | bytes 27656 | tf_op jit(solution)/shard_map/ppermute | solution.py:34
  176.7 3.7 %collective-permute-start = (bf16[9,16,32]{2,1,0:T(8,128)(2,1)S(1)}, bf16[9,16,32]{2,1,0:T(8,128)(2,1)S(1)}, u32[]{:S(2)}, u32[]{:S(2)}) collective-permute-start(bf16[9,16,32]{2,1,0:T(8,128)(2,1)S(1)} %get-tuple-element.13), channel_id=1, source_target_pairs={{0,1},{1,2},{2,3},{3,4},{4,5},{5,6},{6,7},{7,0},{8,9},{9,10},{10,1... | collective-permute-start | bytes 27656 | tf_op jit(solution)/shard_map/ppermute | solution.py:31
  180.4 4.6 %collective-permute-done = bf16[9,16,32]{2,1,0:T(8,128)(2,1)S(1)} collective-permute-done((bf16[9,16,32]{2,1,0:T(8,128)(2,1)S(1)}, bf16[9,16,32]{2,1,0:T(8,128)(2,1)S(1)}, u32[]{:S(2)}, u32[]{:S(2)}) %collective-permute-start) | collective-permute-done | bytes 9248 | tf_op jit(solution)/shard_map/ppermute | solution.py:31
  185.0 0.1 maximum_convert_fusion
  185.8 0.5 slice_add_fusion.4
  186.4 0.5 slice_add_fusion.3
  186.9 0.5 slice_add_fusion.2
  187.5 0.5 slice_add_fusion.1
  188.0 0.5 slice_add_fusion
  188.5 0.6 fusion.120
  189.1 0.5 fusion.10
  189.7 0.7 multiply_subtract_fusion
  190.4 0.6 constant_dynamic-update-slice_fusion.53
  191.0 0.6 constant_dynamic-update-slice_fusion.52
  191.7 0.6 constant_dynamic-update-slice_fusion.50
  192.3 0.6 constant_dynamic-update-slice_fusion.49
  192.9 0.6 constant_dynamic-update-slice_fusion.48
  193.5 0.6 constant_dynamic-update-slice_fusion.47
  194.1 0.6 constant_dynamic-update-slice_fusion.46
  194.6 0.6 constant_dynamic-update-slice_fusion.45
  195.3 0.6 fusion.11
  195.9 0.5 copy.23
  196.4 1.4 reshape.157
  197.9 24.3 %all_to_all.47 = f32[64,1,512]{2,1,0:T(1,128)S(1)} all-to-all(f32[64,1,512]{2,1,0:T(1,128)S(1)} %reshape.157), channel_id=1, replica_groups=mesh['band'=64,'tile'=8] {'band'}, dimensions={0} | all-to-all | bytes 262144 | tf_op jit(solution)/shard_map/all_to_all | solution.py:139
  222.2 0.5 broadcast.416
  222.7 0.9 reduce.2
  223.7 1.4 reshape.158
  225.1 0.6 copy.39
  225.7 0.6 all_to_all.40
  226.3 0.1 broadcast_in_dim.9
  226.4 19.3 %all_to_all.48 = f32[8,1024,2,16]{1,3,2,0:T(8,128)S(1)} all-to-all(f32[8,1024,2,16]{1,3,2,0:T(8,128)S(1)} %broadcast_in_dim.9), channel_id=1, replica_groups=mesh['band'=64,'tile'=8] {'tile'}, dimensions={0} | all-to-all | bytes 2097152 | tf_op jit(solution)/shard_map/all_to_all | solution.py:18
  245.8 4.0 %fusion.19 = f32[16,2,128]{2,1,0:T(2,128)} fusion(bf16[16,128,1024]{2,1,0:T(8,128)(2,1)} %param.4, bf16[1024,2,16]{0,2,1:T(8,128)(2,1)S(1)} %reduce_sum.32), kind=kOutput, calls=%fused_computation.85 | convolution fusion | flops 8388608 | bytes 4276224 | tf_op jit(solution)/shard_map/slr,res->sel/dot_general | solution.py:141
  (54 shorter events, 0.5 us)
Async XLA Ops:
  106.1 6.5 %copy-start.1 = (s32[1024]{0:T(1024)S(1)}, s32[1024]{0:T(1024)}, u32[]{:S(2)}) copy-start(s32[1024]{0:T(1024)} %param.5) | copy-start | bytes 12292
  106.1 63.3 %all-to-all-start.1 = ((bf16[8,1024,9,2,1,16]{1,5,4,3,2,0:T(8,128)(2,1)}), bf16[8,1024,9,2,1,16]{1,5,4,3,2,0:T(8,128)(2,1)}, u32[]{:S(2)}, u32[]{:S(2)}) async-start(bf16[8,1024,9,2,1,16]{1,5,4,3,2,0:T(8,128)(2,1)} %broadcast_in_dim.8), calls=%async_computation.1 | async-start | bytes 9437184 | tf_op jit(solution)/shard_map/all_to_all | solution.py:18
  173.4 7.0 %collective-permute-start.1 = (bf16[9,16,32]{2,1,0:T(8,128)(2,1)S(1)}, bf16[9,16,32]{2,1,0:T(8,128)(2,1)S(1)}, u32[]{:S(2)}, u32[]{:S(2)}) collective-permute-start(bf16[9,16,32]{2,1,0:T(8,128)(2,1)S(1)} %get-tuple-element.14), channel_id=1, source_target_pairs={{1,0},{2,1},{3,2},{4,3},{5,4},{6,5},{7,6},{0,7},{9,8},{10,9},{11,1... | collective-permute-start | bytes 27656 | tf_op jit(solution)/shard_map/ppermute | solution.py:34
  176.7 8.3 %collective-permute-start = (bf16[9,16,32]{2,1,0:T(8,128)(2,1)S(1)}, bf16[9,16,32]{2,1,0:T(8,128)(2,1)S(1)}, u32[]{:S(2)}, u32[]{:S(2)}) collective-permute-start(bf16[9,16,32]{2,1,0:T(8,128)(2,1)S(1)} %get-tuple-element.13), channel_id=1, source_target_pairs={{0,1},{1,2},{2,3},{3,4},{4,5},{5,6},{6,7},{7,0},{8,9},{9,10},{10,1... | collective-permute-start | bytes 27656 | tf_op jit(solution)/shard_map/ppermute | solution.py:31
  195.2 1.2 copy-start
where the time goes:
time: 251 us; the launch traced here: 250 us
  blocking collectives  95.7 us (38%)
  local copies, waits for them, and re-layouts  56.4 us (22%)
  waiting for transfers between devices  52.1 us (21%)
  other arithmetic  22.8 us (9%)
  starting transfers between devices  13.5 us (5%)
  matrix products  8.03 us (3%)
    all_to_all x1, blocking collectives, to_band_layout(): lax.all_to_all(parts, 'band', split_axis=3, concat_axis=0, tiled=True)  52 us
    all_to_all x1, waiting for transfers between devices, sent_to_all(): return lax.all_to_all(copies, axis, split_axis=0, concat_axis=0, tiled=True)  47.6 us
    all_to_all x1, blocking collectives, body(): lax.all_to_all(cycle_partial, 'band', split_axis=2, concat_axis=0, tiled=...  24.3 us
    all_to_all x3, local copies, waits for them, and re-layouts, to_band_layout(): lax.all_to_all(parts, 'band', split_axis=3, concat_axis=0, tiled=True)  23.9 us
    all_to_all x1, blocking collectives, sent_to_all(): return lax.all_to_all(copies, axis, split_axis=0, concat_axis=0, tiled=True)  19.3 us
    unnamed x8, local copies, waits for them, and re-layouts  14.2 us
    reshape x2, local copies, waits for them, and re-layouts, body(): partial_value.astype(jnp.bfloat16).reshape(slot_count, C, 2, band_count, RB)  12.5 us
    another operation x1, other arithmetic  9.19 us
  transfers between devices with their start and end apart: 3, of which 2 were waited for; matrix products, arithmetic and copies ran while one was open for 4% of the time, Pallas kernels for 0%

commit v1 on v0

--- a/solution.py
+++ b/solution.py
@@ -136,7 +136,9 @@
     cycle_partial = jnp.einsum(
         "rx,esx->res", map_low, own_basis, preferred_element_type=jnp.float32
     )
-    routed = lax.all_to_all(cycle_partial, "band", split_axis=2, concat_axis=0, tiled=True)
+    shards = jnp.split(cycle_partial, lax.axis_size("band"), axis=2)
+    received = lax.all_to_all(jnp.stack(shards), "band", 0, 0)
+    routed = jnp.concatenate(received, axis=0)
     cycle_spectra = taken_together_2(routed, "tile").astype(jnp.bfloat16)
     ilc_alm = jnp.einsum(
         "slr,res->sel", legendre, cycle_spectra, preferred_element_type=jnp.float32

time: 251 us -> 254 us (1.012)
  local copies, waits for them, and re-layouts: 56.4 us -> 60 us
    unnamed x8 -> x71, local copies, waits for them, and re-layouts: 14.2 us -> 18.5 us
where the time goes in v1:
time: 254 us; the launch traced here: 253 us
  blocking collectives  95.7 us (38%)
  local copies, waits for them, and re-layouts  60 us (24%)
  waiting for transfers between devices  52.1 us (21%)
  other arithmetic  22.8 us (9%)
  starting transfers between devices  13.5 us (5%)
  matrix products  8.03 us (3%)
    all_to_all x1, blocking collectives, to_band_layout(): lax.all_to_all(parts, 'band', split_axis=3, concat_axis=0, tiled=True)  52 us
    all_to_all x1, waiting for transfers between devices, sent_to_all(): return lax.all_to_all(copies, axis, split_axis=0, concat_axis=0, tiled=True)  47.6 us
    all_to_all x1, blocking collectives, body(): received = lax.all_to_all(jnp.stack(shards), 'band', 0, 0)  24.3 us
    all_to_all x3, local copies, waits for them, and re-layouts, to_band_layout(): lax.all_to_all(parts, 'band', split_axis=3, concat_axis=0, tiled=True)  23.9 us
    all_to_all x1, blocking collectives, sent_to_all(): return lax.all_to_all(copies, axis, split_axis=0, concat_axis=0, tiled=True)  19.3 us
    unnamed x71, local copies, waits for them, and re-layouts  18.5 us
    reshape x2, local copies, waits for them, and re-layouts, body(): partial_value.astype(jnp.bfloat16).reshape(slot_count, C, 2, band_count, RB)  12.5 us
    another operation x1, other arithmetic  9.19 us
  transfers between devices with their start and end apart: 3, of which 2 were waited for; matrix products, arithmetic and copies ran while one was open for 4% of the time, Pallas kernels for 0%

profile of v1, /device:TPU:1, one launch (start us, length us, event | category | flops | bytes accessed | tf_op | source)
XLA Modules:
  0.0 253.4 jit_solution(8261705352776086748)
XLA Ops:
  0.6 2.9 %fusion.7 = bf16[16,9,2,1024]{3,1,2,0:T(8,128)(2,1)S(1)} fusion(bf16[16,128,1024]{2,1,0:T(8,128)(2,1)} %param.4, bf16[16,9,2,128]{3,2,1,0:T(2,128)(2,1)} %param.3), kind=kOutput, calls=%fused_computation.20 | convolution fusion | flops 75792384 | bytes 4857856 | tf_op jit(solution)/shard_map/scel,slr->scer/dot_general | solution.py:121
  3.5 4.9 %reshape.158 = bf16[16,9,2,64,16]{4,3,1,2,0:T(8,128)(2,1)} reshape(bf16[16,9,2,1024]{3,1,2,0:T(8,128)(2,1)S(1)} %fusion.7) | data formatting | bytes 1179648 | tf_op jit(solution)/shard_map/reshape | solution.py:123
  8.5 7.5 %copy.169 = bf16[16,9,2,64,16]{4,0,2,1,3:T(8,128)(2,1)} copy(bf16[16,9,2,64,16]{4,3,1,2,0:T(8,128)(2,1)} %reshape.158) | data formatting | bytes 1179648 | tf_op jit(solution)/shard_map/reshape | solution.py:123
  16.0 6.6 %reshape.159 = bf16[64,2,2304]{2,1,0:T(2,128)(2,1)S(1)} reshape(bf16[64,9,2,16,16]{4,3,2,1,0:T(8,128)(2,1)} %bitcast.296) | data formatting | bytes 1179648
  22.6 52.0 %all_to_all.33 = bf16[64,2,2304]{2,1,0:T(2,128)(2,1)S(1)} all-to-all(bf16[64,2,2304]{2,1,0:T(2,128)(2,1)S(1)} %reshape.159), channel_id=1, replica_groups=mesh['band'=64,'tile'=8] {'band'}, dimensions={0} | all-to-all | bytes 1179648 | tf_op jit(solution)/shard_map/all_to_all | solution.py:112
  74.7 4.7 %reshape.160 = bf16[64,9,2,16,16]{4,3,2,1,0:T(8,128)(2,1)} reshape(bf16[64,2,2304]{2,1,0:T(2,128)(2,1)S(1)} %all_to_all.33) | data formatting | bytes 1179648
  79.4 5.3 %bitcast_bitcast_fusion = bf16[64,16,9,2,1,16]{5,1,3,2,0,4:T(8,128)(2,1)} fusion(bf16[64,9,2,16,16]{4,3,2,1,0:T(8,128)(2,1)} %reshape.160), kind=kLoop, calls=%fused_computation.377 | loop fusion | bytes 1179648 | tf_op jit(solution)/shard_map/all_to_all | solution.py:112
  84.7 9.8 %copy.155 = bf16[64,16,9,2,1,16]{1,0,5,3,2,4:T(8,128)(2,1)} copy(bf16[64,16,9,2,1,16]{5,1,3,2,0,4:T(8,128)(2,1)} %bitcast_bitcast_fusion) | data formatting | bytes 1179648 | tf_op jit(solution)/shard_map/all_to_all | solution.py:112
  94.5 8.9 %all_to_all.25 = bf16[1024,9,2,16]{0,3,2,1:T(8,128)(2,1)S(1)} reshape(bf16[64,16,9,2,1,16]{1,0,5,3,2,4:T(8,128)(2,1)} %copy.155) | data formatting | bytes 1179648 | tf_op jit(solution)/shard_map/all_to_all | solution.py:112
  103.3 2.8 %broadcast_in_dim.8 = bf16[8,1024,9,2,1,16]{1,5,4,3,2,0:T(8,128)(2,1)} broadcast(bf16[1024,9,2,16]{0,3,2,1:T(8,128)(2,1)S(1)} %all_to_all.25), dimensions={1,2,3,5} | broadcast | bytes 5308416 | tf_op jit(solution)/shard_map/broadcast_in_dim | solution.py:17
  106.1 6.5 %all-to-all-start.1 = ((bf16[8,1024,9,2,1,16]{1,5,4,3,2,0:T(8,128)(2,1)}), bf16[8,1024,9,2,1,16]{1,5,4,3,2,0:T(8,128)(2,1)}, u32[]{:S(2)}, u32[]{:S(2)}) async-start(bf16[8,1024,9,2,1,16]{1,5,4,3,2,0:T(8,128)(2,1)} %broadcast_in_dim.8), calls=%async_computation.1 | async-start | bytes 9437184 | tf_op jit(solution)/shard_map/all_to_all | solution.py:18
  112.6 9.2 %multiply_convert_fusion.1 = (bf16[1,1024,512]{2,1,0:T(8,128)(2,1)S(1)}, bf16[1,1024,512]{2,1,0:T(8,128)(2,1)S(1)}) fusion(s32[512]{0:T(512)S(1)} %iota_add_fusion, s32[1024]{0:T(1024)S(1)} %copy-done.1), kind=kLoop, calls=%fused_computation.14 | loop fusion | flops 9961472 | bytes 2103296 | tf_op jit(solution)/shard_map/convert.1
  121.8 47.6 %all-to-all-done.1 = bf16[8,1024,9,2,1,16]{1,5,4,3,2,0:T(8,128)(2,1)} async-done(((bf16[8,1024,9,2,1,16]{1,5,4,3,2,0:T(8,128)(2,1)}), bf16[8,1024,9,2,1,16]{1,5,4,3,2,0:T(8,128)(2,1)}, u32[]{:S(2)}, u32[]{:S(2)}) %all-to-all-start.1) | async-done | bytes 4718624 | tf_op jit(solution)/shard_map/all_to_all | solution.py:18
  169.4 3.4 %reduce_sum.30 = bf16[1024,9,2,16]{0,3,2,1:T(8,128)(2,1)S(1)} reduce(bf16[8,1024,9,2,1,16]{1,5,4,3,2,0:T(8,128)(2,1)} %all-to-all-done.1, bf16[]{:T(256)} %constant.12.clone.1), dimensions={0,4}, to_apply=%region_0.1 | reduce | flops 2064384 | bytes 5308418 | tf_op jit(solution)/shard_map/reduce_sum | solution.py:22
  172.8 0.5 fusion.15
  173.3 0.1 fusion.121
  173.4 3.3 %collective-permute-start.1 = (bf16[9,16,32]{2,1,0:T(8,128)(2,1)S(1)}, bf16[9,16,32]{2,1,0:T(8,128)(2,1)S(1)}, u32[]{:S(2)}, u32[]{:S(2)}) collective-permute-start(bf16[9,16,32]{2,1,0:T(8,128)(2,1)S(1)} %get-tuple-element.14), channel_id=1, source_target_pairs={{1,0},{2,1},{3,2},{4,3},{5,4},{6,5},{7,6},{0,7},{9,8},{10,9},{11,1... | collective-permute-start | bytes 27656 | tf_op jit(solution)/shard_map/ppermute | solution.py:34
  176.7 3.7 %collective-permute-start = (bf16[9,16,32]{2,1,0:T(8,128)(2,1)S(1)}, bf16[9,16,32]{2,1,0:T(8,128)(2,1)S(1)}, u32[]{:S(2)}, u32[]{:S(2)}) collective-permute-start(bf16[9,16,32]{2,1,0:T(8,128)(2,1)S(1)} %get-tuple-element.13), channel_id=1, source_target_pairs={{0,1},{1,2},{2,3},{3,4},{4,5},{5,6},{6,7},{7,0},{8,9},{9,10},{10,1... | collective-permute-start | bytes 27656 | tf_op jit(solution)/shard_map/ppermute | solution.py:31
  180.4 4.6 %collective-permute-done = bf16[9,16,32]{2,1,0:T(8,128)(2,1)S(1)} collective-permute-done((bf16[9,16,32]{2,1,0:T(8,128)(2,1)S(1)}, bf16[9,16,32]{2,1,0:T(8,128)(2,1)S(1)}, u32[]{:S(2)}, u32[]{:S(2)}) %collective-permute-start) | collective-permute-done | bytes 9248 | tf_op jit(solution)/shard_map/ppermute | solution.py:31
  185.0 0.1 maximum_convert_fusion
  185.8 0.5 slice_add_fusion.4
  186.4 0.5 slice_add_fusion.3
  186.9 0.5 slice_add_fusion.2
  187.5 0.5 slice_add_fusion.1
  188.0 0.5 slice_add_fusion
  188.5 0.6 fusion.120
  189.1 0.5 fusion.10
  189.7 0.7 multiply_subtract_fusion
  190.4 0.6 constant_dynamic-update-slice_fusion.53
  191.0 0.6 constant_dynamic-update-slice_fusion.52
  191.7 0.6 constant_dynamic-update-slice_fusion.50
  192.3 0.6 constant_dynamic-update-slice_fusion.49
  192.9 0.6 constant_dynamic-update-slice_fusion.48
  193.5 0.6 constant_dynamic-update-slice_fusion.47
  194.1 0.6 constant_dynamic-update-slice_fusion.46
  194.6 0.6 constant_dynamic-update-slice_fusion.45
  195.3 0.6 fusion.11
  195.9 0.1 constant_dynamic-update-slice_fusion.116
  200.1 0.6 copy.156
  200.6 1.7 reshape.161
  202.3 24.3 %all_to_all.34 = f32[64,1,512]{2,1,0:T(1,128)S(1)} all-to-all(f32[64,1,512]{2,1,0:T(1,128)S(1)} %reshape.161), channel_id=1, replica_groups=mesh['band'=64,'tile'=8] {'band'}, dimensions={0} | all-to-all | bytes 262144 | tf_op jit(solution)/shard_map/all_to_all | solution.py:140
  226.6 0.5 broadcast.416
  227.2 0.9 reduce.2
  228.1 1.4 reshape.162
  229.5 0.4 copy.163
  229.9 0.1 broadcast_in_dim.9
  230.1 19.3 %all_to_all.35 = f32[8,1024,2,16]{1,3,2,0:T(8,128)S(1)} all-to-all(f32[8,1024,2,16]{1,3,2,0:T(8,128)S(1)} %broadcast_in_dim.9), channel_id=1, replica_groups=mesh['band'=64,'tile'=8] {'tile'}, dimensions={0} | all-to-all | bytes 2097152 | tf_op jit(solution)/shard_map/all_to_all | solution.py:18
  249.5 4.0 %fusion.19 = f32[16,2,128]{2,1,0:T(2,128)} fusion(bf16[16,128,1024]{2,1,0:T(8,128)(2,1)} %param.4, bf16[1024,2,16]{0,2,1:T(8,128)(2,1)S(1)} %reduce_sum.32), kind=kOutput, calls=%fused_computation.148 | convolution fusion | flops 8388608 | bytes 4276224 | tf_op jit(solution)/shard_map/slr,res->sel/dot_general | solution.py:143
  (117 shorter events, 4.6 us)
Async XLA Ops:
  106.1 6.5 %copy-start.1 = (s32[1024]{0:T(1024)S(1)}, s32[1024]{0:T(1024)}, u32[]{:S(2)}) copy-start(s32[1024]{0:T(1024)} %param.5) | copy-start | bytes 12292
  106.1 63.3 %all-to-all-start.1 = ((bf16[8,1024,9,2,1,16]{1,5,4,3,2,0:T(8,128)(2,1)}), bf16[8,1024,9,2,1,16]{1,5,4,3,2,0:T(8,128)(2,1)}, u32[]{:S(2)}, u32[]{:S(2)}) async-start(bf16[8,1024,9,2,1,16]{1,5,4,3,2,0:T(8,128)(2,1)} %broadcast_in_dim.8), calls=%async_computation.1 | async-start | bytes 9437184 | tf_op jit(solution)/shard_map/all_to_all | solution.py:18
  173.4 7.0 %collective-permute-start.1 = (bf16[9,16,32]{2,1,0:T(8,128)(2,1)S(1)}, bf16[9,16,32]{2,1,0:T(8,128)(2,1)S(1)}, u32[]{:S(2)}, u32[]{:S(2)}) collective-permute-start(bf16[9,16,32]{2,1,0:T(8,128)(2,1)S(1)} %get-tuple-element.14), channel_id=1, source_target_pairs={{1,0},{2,1},{3,2},{4,3},{5,4},{6,5},{7,6},{0,7},{9,8},{10,9},{11,1... | collective-permute-start | bytes 27656 | tf_op jit(solution)/shard_map/ppermute | solution.py:34
  176.7 8.3 %collective-permute-start = (bf16[9,16,32]{2,1,0:T(8,128)(2,1)S(1)}, bf16[9,16,32]{2,1,0:T(8,128)(2,1)S(1)}, u32[]{:S(2)}, u32[]{:S(2)}) collective-permute-start(bf16[9,16,32]{2,1,0:T(8,128)(2,1)S(1)} %get-tuple-element.13), channel_id=1, source_target_pairs={{0,1},{1,2},{2,3},{3,4},{4,5},{5,6},{6,7},{7,0},{8,9},{9,10},{10,1... | collective-permute-start | bytes 27656 | tf_op jit(solution)/shard_map/ppermute | solution.py:31
  195.2 1.9 copy-start
